TPU v7x, 128 devices: a whole 4x4x4 slice. The times are simulated.
128 devices in a mesh: dom: 32 (over y, x, core), near: 4 (over z).
Axes of the slice: x: 4, y: 4, z: 4, core: 2. Of those that a mesh axis runs over, the one named last changes fastest.
Arguments:
- start_block: float32 [131072, 128], P(('dom', 'near')), may hold values from -6 to 6
- near_tiles: float32 [6144, 128, 128], P(('dom', 'near')), may hold values from -0.09375 to 0.09375
- near_src: int32 [6144], P(('dom', 'near')), may hold values from 0 to 31, as said below
- near_mask: int32 [6144], P(('dom', 'near')), may hold values 0 or 1
- far_tiles: float32 [1024, 128, 128], P(('dom', 'near')), may hold values from -0.09375 to 0.09375
- far_src: int32 [1024], P(('dom', 'near')), may hold values from 0 to 31
- far_mask: int32 [1024], P(('dom', 'near')), may hold values 0 or 1
- bound_count: int32 [128], P(('dom', 'near')), may hold values from 1 to 128
Outputs:
- encodings: float32 [131072, 128], P(('dom', 'near'))
- rayleigh: float32 [128, 128], replicated
Inputs may be any that keep to these rules, and one draw needn't show every extreme that they name: `near_src`: each partition holds 48 consecutive slots; the slot at position j among them (j from 0) lies in tile row j // 6; the first slot of each tile row reads the partition's own tile of that row; every source tile from another partition of the group is one of that partition's first 4 tiles.
All inputs are finite; a program needn't handle non-finite values. No bound on the sum of `near_mask` or of `far_mask` on one device may be relied on, other than what follows from the above.
Results may differ from a plain program's by a relative error of at most 0.0003.
Values sent between devices are 32-bit elements; how exact they have to be, the bound alone decides.
No kernel may reach another device: no remote copies, remote signals or barrier semaphores. Data moves between devices by JAX's collectives and lax.ppermute only.
A program may use at most 64 MiB of HBM per device.

v0:
```python
from functools import partial
import jax
import jax.numpy as jnp
from jax import lax
from jax.sharding import PartitionSpec as P

NPER = 6
ITERS = 2
DEG = 3
LOWER_EDGE = 0.6
UPPER_EDGE = 2.0


def apply_operator(
    block, near_tiles, near_src, near_mask, far_tiles, far_src, far_mask, bound_count
):
    tile_rows = near_tiles.shape[1]
    width = block.shape[1]
    tiles_dev = block.shape[0] // tile_rows
    group_size = lax.axis_size("near")
    gathered = lax.all_gather(block, "near", axis=0, tiled=True)
    picked = gathered.reshape(group_size * tiles_dev, tile_rows, width)[near_src]
    products = jnp.einsum("sij,sjk->sik", near_tiles, picked, precision=lax.Precision.HIGHEST)
    products = products * near_mask.astype(jnp.float32)[:, None, None]
    near_sum = products.reshape(tiles_dev, NPER, tile_rows, width).sum(axis=1)
    limit = (jnp.arange(tile_rows) < bound_count[0]).astype(jnp.float32)
    edge_tile = block[:tile_rows] * limit[:, None]
    edges = lax.all_gather(edge_tile, "dom", axis=0, tiled=True).reshape(
        lax.axis_size("dom"), tile_rows, width
    )
    far_pick = edges[far_src]
    far_sum = jnp.einsum("sij,sjk->sik", far_tiles, far_pick, precision=lax.Precision.HIGHEST)
    far_sum = far_sum * far_mask.astype(jnp.float32)[:, None, None]
    return block - (near_sum + far_sum).reshape(block.shape)


def chebyshev(current, image, operator):
    center = (UPPER_EDGE + LOWER_EDGE) / 2.0
    half = (UPPER_EDGE - LOWER_EDGE) / 2.0
    previous = current
    present = (image - center * current) / half
    for degree in range(DEG - 1):
        following = 2.0 * (operator(present) - center * present) / half - previous
        previous, present = (present, following)
    return present


def inner(left, right):
    return jnp.dot(
        left.T, right, precision=lax.Precision.HIGHEST, preferred_element_type=jnp.float32
    )


def times_inverse(block, lower_inv):
    return jnp.dot(
        block, lower_inv.T, precision=lax.Precision.HIGHEST, preferred_element_type=jnp.float32
    )


def inverse_factor(gram):
    lower = jnp.linalg.cholesky(gram)
    return jax.scipy.linalg.solve_triangular(
        lower, jnp.eye(gram.shape[0], dtype=jnp.float32), lower=True
    )


def local(start_block, near_tiles, near_src, near_mask, far_tiles, far_src, far_mask, bound_count):
    operator = partial(
        apply_operator,
        near_tiles=near_tiles,
        near_src=near_src,
        near_mask=near_mask,
        far_tiles=far_tiles,
        far_src=far_src,
        far_mask=far_mask,
        bound_count=bound_count,
    )
    nodes_all = start_block.shape[0] * lax.axis_size("dom") * lax.axis_size("near")
    current = start_block
    image = operator(current)
    for iteration in range(ITERS):
        if iteration > 0:
            image = operator(current)
        filtered = chebyshev(current, image, operator)
        gram = lax.psum(inner(filtered, filtered), ("dom", "near")) / nodes_all
        lower_inv = inverse_factor(gram)
        current = times_inverse(filtered, lower_inv)
    final_image = operator(current)
    rayleigh = lax.psum(inner(current, final_image), ("dom", "near")) / nodes_all
    return (current, rayleigh)


def solution(mesh):
    return jax.shard_map(
        local,
        mesh=mesh,
        in_specs=(
            P(("dom", "near"), None),
            P(("dom", "near"), None, None),
            P(("dom", "near")),
            P(("dom", "near")),
            P(("dom", "near"), None, None),
            P(("dom", "near")),
            P(("dom", "near")),
            P(("dom", "near")),
        ),
        out_specs=(P(("dom", "near"), None), P()),
        check_vma=False,
    )
```

profile of v0, /device:TPU:1, one launch (start us, length us, event | category | flops | bytes accessed | tf_op | source)
XLA Modules:
  0.0 1082.7 jit_solution(1137057290617790462)
XLA Ops:
  13.1 30.7 %all-gather.15.cloned.1.call-done = f32[4096,128]{1,0:T(8,128)} async-done(((f32[1024,128]{1,0:T(8,128)}), f32[4096,128]{1,0:T(8,128)}) %all-gather.15.cloned.1.call-update) | async-done | bytes 2097168 | tf_op jit(solution)/shard_map/all_gather | solution.py:21
  47.7 8.1 convolution_multiply_fusion.6
  60.8 29.6 %all-gather.17.cloned.1.call-done = f32[4096,128]{1,0:T(8,128)} async-done(((f32[128,128]{1,0:T(8,128)}), f32[4096,128]{1,0:T(8,128)}) %all-gather.17.cloned.1.call-update) | async-done | bytes 2097168 | tf_op jit(solution)/shard_map/all_gather | solution.py:28
  99.8 28.3 %all-gather.19.cloned.1.call-done = f32[4096,128]{1,0:T(8,128)} async-done(((f32[1024,128]{1,0:T(8,128)}), f32[4096,128]{1,0:T(8,128)}) %all-gather.19.cloned.1.call-update) | async-done | bytes 2097168 | tf_op jit(solution)/shard_map/all_gather | solution.py:21
  145.2 29.5 %all-gather.21.cloned.1.call-done = f32[4096,128]{1,0:T(8,128)} async-done(((f32[128,128]{1,0:T(8,128)}), f32[4096,128]{1,0:T(8,128)}) %all-gather.21.cloned.1.call-update) | async-done | bytes 2097168 | tf_op jit(solution)/shard_map/all_gather | solution.py:28
  184.5 28.1 %all-gather.23.cloned.1.call-done = f32[4096,128]{1,0:T(8,128)} async-done(((f32[1024,128]{1,0:T(8,128)}), f32[4096,128]{1,0:T(8,128)}) %all-gather.23.cloned.1.call-update) | async-done | bytes 2097168 | tf_op jit(solution)/shard_map/all_gather | solution.py:21
  216.5 8.1 convolution_multiply_fusion.4
  229.7 29.5 %all-gather.25.cloned.1.call-done = f32[4096,128]{1,0:T(8,128)} async-done(((f32[128,128]{1,0:T(8,128)}), f32[4096,128]{1,0:T(8,128)}) %all-gather.25.cloned.1.call-update) | async-done | bytes 2097168 | tf_op jit(solution)/shard_map/all_gather | solution.py:28
  268.2 138.8 %all-reduce.4.cloned.1.call-done = f32[128,128]{0,1:T(8,128)} async-done(((f32[128,128]{0,1:T(8,128)}), f32[128,128]{0,1:T(8,128)}) %all-reduce.4.cloned.1.call-update) | async-done | bytes 65552 | tf_op jit(solution)/shard_map/psum | solution.py:85
  408.8 11.7 %cholesky.44 = f32[128,128]{1,0:T(8,128)S(1)} custom-call(f32[128,128]{1,0:T(8,128)S(1)} %fusion.41), custom_call_target="Cholesky" | custom-call | tf_op jit(solution)/shard_map/jit(cholesky)/cholesky | solution.py:61
  421.9 9.8 custom-call.6
  436.1 26.2 %all-gather.27.cloned.1.call-done = f32[4096,128]{1,0:T(8,128)} async-done(((f32[1024,128]{1,0:T(8,128)}), f32[4096,128]{1,0:T(8,128)}) %all-gather.27.cloned.1.call-update) | async-done | bytes 2097168 | tf_op jit(solution)/shard_map/all_gather | solution.py:21
  466.3 8.1 convolution_multiply_fusion.3
  479.4 29.6 %all-gather.29.cloned.1.call-done = f32[4096,128]{1,0:T(8,128)} async-done(((f32[128,128]{1,0:T(8,128)}), f32[4096,128]{1,0:T(8,128)}) %all-gather.29.cloned.1.call-update) | async-done | bytes 2097168 | tf_op jit(solution)/shard_map/all_gather | solution.py:28
  518.6 28.1 %all-gather.31.cloned.1.call-done = f32[4096,128]{1,0:T(8,128)} async-done(((f32[1024,128]{1,0:T(8,128)}), f32[4096,128]{1,0:T(8,128)}) %all-gather.31.cloned.1.call-update) | async-done | bytes 2097168 | tf_op jit(solution)/shard_map/all_gather | solution.py:21
  563.8 29.6 %all-gather.33.cloned.1.call-done = f32[4096,128]{1,0:T(8,128)} async-done(((f32[128,128]{1,0:T(8,128)}), f32[4096,128]{1,0:T(8,128)}) %all-gather.33.cloned.1.call-update) | async-done | bytes 2097168 | tf_op jit(solution)/shard_map/all_gather | solution.py:28
  603.0 28.3 %all-gather.35.cloned.1.call-done = f32[4096,128]{1,0:T(8,128)} async-done(((f32[1024,128]{1,0:T(8,128)}), f32[4096,128]{1,0:T(8,128)}) %all-gather.35.cloned.1.call-update) | async-done | bytes 2097168 | tf_op jit(solution)/shard_map/all_gather | solution.py:21
  648.4 29.6 %all-gather.37.cloned.1.call-done = f32[4096,128]{1,0:T(8,128)} async-done(((f32[128,128]{1,0:T(8,128)}), f32[4096,128]{1,0:T(8,128)}) %all-gather.37.cloned.1.call-update) | async-done | bytes 2097168 | tf_op jit(solution)/shard_map/all_gather | solution.py:28
  687.5 138.4 %all-reduce.6.cloned.1.call-done = f32[128,128]{0,1:T(8,128)} async-done(((f32[128,128]{0,1:T(8,128)}), f32[128,128]{0,1:T(8,128)}) %all-reduce.6.cloned.1.call-update) | async-done | bytes 65552 | tf_op jit(solution)/shard_map/psum | solution.py:85
  827.7 11.7 %cholesky.55 = f32[128,128]{1,0:T(8,128)S(1)} custom-call(f32[128,128]{1,0:T(8,128)S(1)} %fusion.39), custom_call_target="Cholesky" | custom-call | tf_op jit(solution)/shard_map/jit(cholesky)/cholesky | solution.py:61
  840.8 9.8 custom-call.7
  855.2 26.0 %all-gather.39.cloned.1.call-done = f32[4096,128]{1,0:T(8,128)} async-done(((f32[1024,128]{1,0:T(8,128)}), f32[4096,128]{1,0:T(8,128)}) %all-gather.39.cloned.1.call-update) | async-done | bytes 2097168 | tf_op jit(solution)/shard_map/all_gather | solution.py:21
  898.3 29.5 %all-gather.41.cloned.1.call-done = f32[4096,128]{1,0:T(8,128)} async-done(((f32[128,128]{1,0:T(8,128)}), f32[4096,128]{1,0:T(8,128)}) %all-gather.41.cloned.1.call-update) | async-done | bytes 2097168 | tf_op jit(solution)/shard_map/all_gather | solution.py:28
  935.5 138.9 %all-reduce.8.cloned.1.call-done = f32[128,128]{0,1:T(8,128)} async-done(((f32[128,128]{0,1:T(8,128)}), f32[128,128]{0,1:T(8,128)}) %all-reduce.8.cloned.1.call-update) | async-done | bytes 65552 | tf_op jit(solution)/shard_map/psum | solution.py:89
  (128 shorter events, 181.6 us)
Async XLA Ops:
  7.2 40.5 %copy-start = (f32[48,128,128]{2,1,0:T(8,128)S(1)}, f32[48,128,128]{2,1,0:T(8,128)}, u32[]{:S(2)}) copy-start(f32[48,128,128]{2,1,0:T(8,128)} %param.12) | copy-start | bytes 9437188
  7.2 36.5 %all-gather.15.cloned.1.call-start = ((), (), s32[]{:S(2)}) async-start(), calls=%async_computation | async-start | bytes 2621440 | tf_op jit(solution)/shard_map/all_gather | solution.py:21
  7.9 82.5 %all-gather.17.cloned.1.call-start = ((), (), s32[]{:S(2)}) async-start(), calls=%async_computation.1 | async-start | bytes 2162688 | tf_op jit(solution)/shard_map/all_gather | solution.py:28
  10.4 117.7 %all-gather.19.cloned.1.call-start = ((), (), s32[]{:S(2)}) async-start(), calls=%async_computation.2 | async-start | bytes 2621440 | tf_op jit(solution)/shard_map/all_gather | solution.py:21
  95.4 0.8 copy-start.2
  98.1 76.5 %all-gather.21.cloned.1.call-start = ((), (), s32[]{:S(2)}) async-start(), calls=%async_computation.3 | async-start | bytes 2162688 | tf_op jit(solution)/shard_map/all_gather | solution.py:28
  99.8 112.8 %all-gather.23.cloned.1.call-start = ((), (), s32[]{:S(2)}) async-start(), calls=%async_computation.4 | async-start | bytes 2621440 | tf_op jit(solution)/shard_map/all_gather | solution.py:21
  179.6 0.8 copy-start.6
  182.6 76.5 %all-gather.25.cloned.1.call-start = ((), (), s32[]{:S(2)}) async-start(), calls=%async_computation.5 | async-start | bytes 2162688 | tf_op jit(solution)/shard_map/all_gather | solution.py:28
  184.2 222.8 %all-reduce.4.cloned.1.call-start = ((), (), s32[]{:S(2)}) async-start(), calls=%async_computation.6 | async-start | bytes 131072 | tf_op jit(solution)/shard_map/psum | solution.py:85
  265.7 0.8 copy-start.4
  268.1 194.2 %all-gather.27.cloned.1.call-start = ((), (), s32[]{:S(2)}) async-start(), calls=%async_computation.7 | async-start | bytes 2621440 | tf_op jit(solution)/shard_map/all_gather | solution.py:21
  434.5 74.6 %all-gather.29.cloned.1.call-start = ((), (), s32[]{:S(2)}) async-start(), calls=%async_computation.8 | async-start | bytes 2162688 | tf_op jit(solution)/shard_map/all_gather | solution.py:28
  436.1 110.6 %all-gather.31.cloned.1.call-start = ((), (), s32[]{:S(2)}) async-start(), calls=%async_computation.9 | async-start | bytes 2621440 | tf_op jit(solution)/shard_map/all_gather | solution.py:21
  514.0 0.8 copy-start.1
  516.7 76.7 %all-gather.33.cloned.1.call-start = ((), (), s32[]{:S(2)}) async-start(), calls=%async_computation.10 | async-start | bytes 2162688 | tf_op jit(solution)/shard_map/all_gather | solution.py:28
  518.4 112.9 %all-gather.35.cloned.1.call-start = ((), (), s32[]{:S(2)}) async-start(), calls=%async_computation.11 | async-start | bytes 2621440 | tf_op jit(solution)/shard_map/all_gather | solution.py:21
  598.3 0.8 copy-start.5
  601.3 76.7 %all-gather.37.cloned.1.call-start = ((), (), s32[]{:S(2)}) async-start(), calls=%async_computation.12 | async-start | bytes 2162688 | tf_op jit(solution)/shard_map/all_gather | solution.py:28
  603.0 223.0 %all-reduce.6.cloned.1.call-start = ((), (), s32[]{:S(2)}) async-start(), calls=%async_computation.13 | async-start | bytes 131072 | tf_op jit(solution)/shard_map/psum | solution.py:85
  684.6 0.8 copy-start.3
  687.0 194.1 %all-gather.39.cloned.1.call-start = ((), (), s32[]{:S(2)}) async-start(), calls=%async_computation.14 | async-start | bytes 2621440 | tf_op jit(solution)/shard_map/all_gather | solution.py:21
  853.3 74.4 %all-gather.41.cloned.1.call-start = ((), (), s32[]{:S(2)}) async-start(), calls=%async_computation.15 | async-start | bytes 2162688 | tf_op jit(solution)/shard_map/all_gather | solution.py:28
  855.0 219.5 %all-reduce.8.cloned.1.call-start = ((), (), s32[]{:S(2)}) async-start(), calls=%async_computation.16 | async-start | bytes 131072 | tf_op jit(solution)/shard_map/psum | solution.py:89
Sparse Core Ops, SparseCore 0:
  9.6 34.0 all-gather.14
  46.5 43.8 all-gather.16
  98.3 29.7 all-gather.18
  130.8 43.8 all-gather.20
  182.7 29.7 all-gather.22
  215.2 43.8 all-gather.24
  268.3 138.7 all-reduce.3
  434.6 27.6 all-gather.26
  465.1 43.8 all-gather.28
  516.9 29.7 all-gather.30
  549.5 43.8 all-gather.32
  601.5 29.7 all-gather.34
  634.1 43.8 all-gather.36
  687.1 138.7 all-reduce.5
  853.4 27.6 all-gather.38
  883.9 43.8 all-gather.40
  935.7 138.7 all-reduce.7
where the time goes:
time: 1090 us; the launch traced here: 1080 us
  waiting for transfers between devices  819 us (75%)
  other arithmetic  95.5 us (9%)
  matrix products  82.2 us (8%)
  local copies, waits for them, and re-layouts  68.7 us (6%)
  between operations  15.2 us (1%)
    psum x2, waiting for transfers between devices, local(): gram = lax.psum(inner(filtered, filtered), ('dom', 'near')) / nodes_all  277 us
    all_gather x7, waiting for transfers between devices, apply_operator(): lax.all_gather(edge_tile, 'dom', axis=0, tiled=True)  207 us
    all_gather x7, waiting for transfers between devices, apply_operator(): gathered = lax.all_gather(block, 'near', axis=0, tiled=True)  196 us
    psum x1, waiting for transfers between devices, local(): lax.psum(inner(current, final_image), ('dom', 'near')) / nodes_all  139 us
    dot_general x7, matrix products, apply_operator(): jnp.einsum('sij,sjk->sik', near_tiles, picked, precision=lax.Precision.HI...  56.9 us
    gather x7, local copies, waits for them, and re-layouts, apply_operator(): gathered.reshape(group_size * tiles_dev, tile_rows, width)[near_src]  28 us
    another operation x6, other arithmetic, inverse_factor(): lower = jnp.linalg.cholesky(gram)  24.8 us
  transfers between devices with their start and end apart: 17, of which 17 were waited for; matrix products, arithmetic and copies ran while one was open for 12% of the time, Pallas kernels for 0%

commit v1 on v0

--- a/solution.py
+++ b/solution.py
@@ -82,7 +82,9 @@
         if iteration > 0:
             image = operator(current)
         filtered = chebyshev(current, image, operator)
-        gram = lax.psum(inner(filtered, filtered), ("dom", "near")) / nodes_all
+        gram = (
+            jnp.sum(lax.all_gather(inner(filtered, filtered), ("dom", "near")), axis=0) / nodes_all
+        )
         lower_inv = inverse_factor(gram)
         current = times_inverse(filtered, lower_inv)
     final_image = operator(current)

time: 1090 us -> 958 us (0.88)
  waiting for transfers between devices: 819 us -> 681 us
    psum x2 -> x0, waiting for transfers between devices: 277 us -> none  [local(): gram = lax.psum(inner(filtered, filtered), ('dom', 'near')) / nodes_all]
    all_gather x0 -> x2, waiting for transfers between devices: none -> 138 us  [local(): lax.all_gather(inner(filtered, filtered), ('dom', 'near'))]
  transfers between devices with their start and end apart: 17 -> 17, of which waited for: 17 -> 17; matrix products, arithmetic and copies ran while one was open for 12% -> 14% of each run, Pallas kernels for 0% -> 0%
where the time goes in v1:
time: 958 us; the launch traced here: 949 us
  waiting for transfers between devices  681 us (71%)
  other arithmetic  99.8 us (10%)
  matrix products  82.4 us (9%)
  local copies, waits for them, and re-layouts  68.9 us (7%)
  between operations  15.2 us (2%)
    all_gather x7, waiting for transfers between devices, apply_operator(): lax.all_gather(edge_tile, 'dom', axis=0, tiled=True)  207 us
    all_gather x7, waiting for transfers between devices, apply_operator(): gathered = lax.all_gather(block, 'near', axis=0, tiled=True)  196 us
    psum x1, waiting for transfers between devices, local(): lax.psum(inner(current, final_image), ('dom', 'near')) / nodes_all  139 us
    all_gather x2, waiting for transfers between devices, local(): lax.all_gather(inner(filtered, filtered), ('dom', 'near'))  138 us
    dot_general x7, matrix products, apply_operator(): jnp.einsum('sij,sjk->sik', near_tiles, picked, precision=lax.Precision.HI...  56.9 us
    gather x7, local copies, waits for them, and re-layouts, apply_operator(): gathered.reshape(group_size * tiles_dev, tile_rows, width)[near_src]  28 us
    another operation x6, other arithmetic, inverse_factor(): lower = jnp.linalg.cholesky(gram)  24.8 us
    another operation x4, other arithmetic, inverse_factor(): jax.scipy.linalg.solve_triangular(lower, jnp.eye(gram.shape[0], dtype=jnp...  20.9 us
  transfers between devices with their start and end apart: 17, of which 17 were waited for; matrix products, arithmetic and copies ran while one was open for 14% of the time, Pallas kernels for 0%

profile of v1, /device:TPU:1, one launch (start us, length us, event | category | flops | bytes accessed | tf_op | source)
XLA Modules:
  0.0 948.6 jit_solution(16330644560165329902)
XLA Ops:
  13.1 30.7 %all-gather.19.cloned.1.call-done = f32[4096,128]{1,0:T(8,128)} async-done(((f32[1024,128]{1,0:T(8,128)}), f32[4096,128]{1,0:T(8,128)}) %all-gather.19.cloned.1.call-update) | async-done | bytes 2097168 | tf_op jit(solution)/shard_map/all_gather | solution.py:21
  47.7 8.1 convolution_multiply_fusion.6
  60.8 29.6 %all-gather.21.cloned.1.call-done = f32[4096,128]{1,0:T(8,128)} async-done(((f32[128,128]{1,0:T(8,128)}), f32[4096,128]{1,0:T(8,128)}) %all-gather.21.cloned.1.call-update) | async-done | bytes 2097168 | tf_op jit(solution)/shard_map/all_gather | solution.py:28
  99.8 28.3 %all-gather.23.cloned.1.call-done = f32[4096,128]{1,0:T(8,128)} async-done(((f32[1024,128]{1,0:T(8,128)}), f32[4096,128]{1,0:T(8,128)}) %all-gather.23.cloned.1.call-update) | async-done | bytes 2097168 | tf_op jit(solution)/shard_map/all_gather | solution.py:21
  145.2 29.5 %all-gather.25.cloned.1.call-done = f32[4096,128]{1,0:T(8,128)} async-done(((f32[128,128]{1,0:T(8,128)}), f32[4096,128]{1,0:T(8,128)}) %all-gather.25.cloned.1.call-update) | async-done | bytes 2097168 | tf_op jit(solution)/shard_map/all_gather | solution.py:28
  184.5 28.1 %all-gather.27.cloned.1.call-done = f32[4096,128]{1,0:T(8,128)} async-done(((f32[1024,128]{1,0:T(8,128)}), f32[4096,128]{1,0:T(8,128)}) %all-gather.27.cloned.1.call-update) | async-done | bytes 2097168 | tf_op jit(solution)/shard_map/all_gather | solution.py:21
  216.5 8.1 convolution_multiply_fusion.4
  229.7 29.5 %all-gather.29.cloned.1.call-done = f32[4096,128]{1,0:T(8,128)} async-done(((f32[128,128]{1,0:T(8,128)}), f32[4096,128]{1,0:T(8,128)}) %all-gather.29.cloned.1.call-update) | async-done | bytes 2097168 | tf_op jit(solution)/shard_map/all_gather | solution.py:28
  268.2 69.2 %all-gather.47.cloned.1.call-done = f32[16384,128]{1,0:T(8,128)} async-done(((f32[128,128]{1,0:T(8,128)}), f32[16384,128]{1,0:T(8,128)}) %all-gather.47.cloned.1.call-update) | async-done | bytes 8388624 | tf_op jit(solution)/shard_map/all_gather | solution.py:86
  341.4 11.7 %cholesky.44 = f32[128,128]{1,0:T(8,128)S(1)} custom-call(f32[128,128]{1,0:T(8,128)S(1)} %fusion.41), custom_call_target="Cholesky" | custom-call | tf_op jit(solution)/shard_map/jit(cholesky)/cholesky | solution.py:61
  354.5 9.8 %custom-call.6 = f32[1,128,128]{1,2,0:T(8,128)S(1)} custom-call(f32[1,128,128]{2,1,0:T(8,128)S(1)} %fusion.36), custom_call_target="InvertDiagBlocksLowerTriangular" | custom-call | tf_op jit(solution)/shard_map/jit(_solve_triangular)/triangular_solve | solution.py:62
  368.7 26.4 %all-gather.31.cloned.1.call-done = f32[4096,128]{1,0:T(8,128)} async-done(((f32[1024,128]{1,0:T(8,128)}), f32[4096,128]{1,0:T(8,128)}) %all-gather.31.cloned.1.call-update) | async-done | bytes 2097168 | tf_op jit(solution)/shard_map/all_gather | solution.py:21
  412.2 29.6 %all-gather.33.cloned.1.call-done = f32[4096,128]{1,0:T(8,128)} async-done(((f32[128,128]{1,0:T(8,128)}), f32[4096,128]{1,0:T(8,128)}) %all-gather.33.cloned.1.call-update) | async-done | bytes 2097168 | tf_op jit(solution)/shard_map/all_gather | solution.py:28
  451.5 28.1 %all-gather.35.cloned.1.call-done = f32[4096,128]{1,0:T(8,128)} async-done(((f32[1024,128]{1,0:T(8,128)}), f32[4096,128]{1,0:T(8,128)}) %all-gather.35.cloned.1.call-update) | async-done | bytes 2097168 | tf_op jit(solution)/shard_map/all_gather | solution.py:21
  483.5 8.1 convolution_multiply_fusion.2
  496.6 29.6 %all-gather.37.cloned.1.call-done = f32[4096,128]{1,0:T(8,128)} async-done(((f32[128,128]{1,0:T(8,128)}), f32[4096,128]{1,0:T(8,128)}) %all-gather.37.cloned.1.call-update) | async-done | bytes 2097168 | tf_op jit(solution)/shard_map/all_gather | solution.py:28
  535.8 28.3 %all-gather.39.cloned.1.call-done = f32[4096,128]{1,0:T(8,128)} async-done(((f32[1024,128]{1,0:T(8,128)}), f32[4096,128]{1,0:T(8,128)}) %all-gather.39.cloned.1.call-update) | async-done | bytes 2097168 | tf_op jit(solution)/shard_map/all_gather | solution.py:21
  581.2 29.6 %all-gather.41.cloned.1.call-done = f32[4096,128]{1,0:T(8,128)} async-done(((f32[128,128]{1,0:T(8,128)}), f32[4096,128]{1,0:T(8,128)}) %all-gather.41.cloned.1.call-update) | async-done | bytes 2097168 | tf_op jit(solution)/shard_map/all_gather | solution.py:28
  620.4 68.8 %all-gather.49.cloned.1.call-done = f32[16384,128]{1,0:T(8,128)} async-done(((f32[128,128]{1,0:T(8,128)}), f32[16384,128]{1,0:T(8,128)}) %all-gather.49.cloned.1.call-update) | async-done | bytes 8388624 | tf_op jit(solution)/shard_map/all_gather | solution.py:86
  693.2 11.7 %cholesky.55 = f32[128,128]{1,0:T(8,128)S(1)} custom-call(f32[128,128]{1,0:T(8,128)S(1)} %fusion.39), custom_call_target="Cholesky" | custom-call | tf_op jit(solution)/shard_map/jit(cholesky)/cholesky | solution.py:61
  706.2 9.8 %custom-call.7 = f32[1,128,128]{1,2,0:T(8,128)S(1)} custom-call(f32[1,128,128]{2,1,0:T(8,128)S(1)} %fusion.37), custom_call_target="InvertDiagBlocksLowerTriangular" | custom-call | tf_op jit(solution)/shard_map/jit(_solve_triangular)/triangular_solve | solution.py:62
  720.6 26.2 %all-gather.43.cloned.1.call-done = f32[4096,128]{1,0:T(8,128)} async-done(((f32[1024,128]{1,0:T(8,128)}), f32[4096,128]{1,0:T(8,128)}) %all-gather.43.cloned.1.call-update) | async-done | bytes 2097168 | tf_op jit(solution)/shard_map/all_gather | solution.py:21
  764.0 29.5 %all-gather.45.cloned.1.call-done = f32[4096,128]{1,0:T(8,128)} async-done(((f32[128,128]{1,0:T(8,128)}), f32[4096,128]{1,0:T(8,128)}) %all-gather.45.cloned.1.call-update) | async-done | bytes 2097168 | tf_op jit(solution)/shard_map/all_gather | solution.py:28
  801.4 138.9 %all-reduce.2.cloned.1.call-done = f32[128,128]{0,1:T(8,128)} async-done(((f32[128,128]{0,1:T(8,128)}), f32[128,128]{0,1:T(8,128)}) %all-reduce.2.cloned.1.call-update) | async-done | bytes 65552 | tf_op jit(solution)/shard_map/psum | solution.py:91
  (132 shorter events, 186.3 us)
Async XLA Ops:
  7.2 40.5 %copy-start = (f32[48,128,128]{2,1,0:T(8,128)S(1)}, f32[48,128,128]{2,1,0:T(8,128)}, u32[]{:S(2)}) copy-start(f32[48,128,128]{2,1,0:T(8,128)} %param.12) | copy-start | bytes 9437188
  7.2 36.5 %all-gather.19.cloned.1.call-start = ((), (), s32[]{:S(2)}) async-start(), calls=%async_computation | async-start | bytes 2621440 | tf_op jit(solution)/shard_map/all_gather | solution.py:21
  7.9 82.5 %all-gather.21.cloned.1.call-start = ((), (), s32[]{:S(2)}) async-start(), calls=%async_computation.1 | async-start | bytes 2162688 | tf_op jit(solution)/shard_map/all_gather | solution.py:28
  10.4 117.7 %all-gather.23.cloned.1.call-start = ((), (), s32[]{:S(2)}) async-start(), calls=%async_computation.2 | async-start | bytes 2621440 | tf_op jit(solution)/shard_map/all_gather | solution.py:21
  95.4 0.8 copy-start.2
  98.1 76.5 %all-gather.25.cloned.1.call-start = ((), (), s32[]{:S(2)}) async-start(), calls=%async_computation.3 | async-start | bytes 2162688 | tf_op jit(solution)/shard_map/all_gather | solution.py:28
  99.8 112.8 %all-gather.27.cloned.1.call-start = ((), (), s32[]{:S(2)}) async-start(), calls=%async_computation.4 | async-start | bytes 2621440 | tf_op jit(solution)/shard_map/all_gather | solution.py:21
  179.6 0.8 copy-start.6
  182.6 76.5 %all-gather.29.cloned.1.call-start = ((), (), s32[]{:S(2)}) async-start(), calls=%async_computation.5 | async-start | bytes 2162688 | tf_op jit(solution)/shard_map/all_gather | solution.py:28
  184.2 153.2 %all-gather.47.cloned.1.call-start = ((), (), s32[]{:S(2)}) async-start(), calls=%async_computation.15 | async-start | bytes 8454144 | tf_op jit(solution)/shard_map/all_gather | solution.py:86
  265.7 0.8 copy-start.4
  268.2 127.0 %all-gather.31.cloned.1.call-start = ((), (), s32[]{:S(2)}) async-start(), calls=%async_computation.6 | async-start | bytes 2621440 | tf_op jit(solution)/shard_map/all_gather | solution.py:21
  367.1 74.8 %all-gather.33.cloned.1.call-start = ((), (), s32[]{:S(2)}) async-start(), calls=%async_computation.7 | async-start | bytes 2162688 | tf_op jit(solution)/shard_map/all_gather | solution.py:28
  368.7 110.8 %all-gather.35.cloned.1.call-start = ((), (), s32[]{:S(2)}) async-start(), calls=%async_computation.8 | async-start | bytes 2621440 | tf_op jit(solution)/shard_map/all_gather | solution.py:21
  446.8 0.8 copy-start.1
  449.6 76.7 %all-gather.37.cloned.1.call-start = ((), (), s32[]{:S(2)}) async-start(), calls=%async_computation.9 | async-start | bytes 2162688 | tf_op jit(solution)/shard_map/all_gather | solution.py:28
  451.2 112.9 %all-gather.39.cloned.1.call-start = ((), (), s32[]{:S(2)}) async-start(), calls=%async_computation.10 | async-start | bytes 2621440 | tf_op jit(solution)/shard_map/all_gather | solution.py:21
  531.2 0.8 copy-start.5
  534.2 76.7 %all-gather.41.cloned.1.call-start = ((), (), s32[]{:S(2)}) async-start(), calls=%async_computation.11 | async-start | bytes 2162688 | tf_op jit(solution)/shard_map/all_gather | solution.py:28
  535.8 153.3 %all-gather.49.cloned.1.call-start = ((), (), s32[]{:S(2)}) async-start(), calls=%async_computation.16 | async-start | bytes 8454144 | tf_op jit(solution)/shard_map/all_gather | solution.py:86
  617.4 0.8 copy-start.3
  619.9 126.9 %all-gather.43.cloned.1.call-start = ((), (), s32[]{:S(2)}) async-start(), calls=%async_computation.12 | async-start | bytes 2621440 | tf_op jit(solution)/shard_map/all_gather | solution.py:21
  718.8 74.7 %all-gather.45.cloned.1.call-start = ((), (), s32[]{:S(2)}) async-start(), calls=%async_computation.13 | async-start | bytes 2162688 | tf_op jit(solution)/shard_map/all_gather | solution.py:28
  720.4 219.9 %all-reduce.2.cloned.1.call-start = ((), (), s32[]{:S(2)}) async-start(), calls=%async_computation.14 | async-start | bytes 131072 | tf_op jit(solution)/shard_map/psum | solution.py:91
Sparse Core Ops, SparseCore 0:
  9.6 34.0 all-gather.18
  46.5 43.8 all-gather.20
  98.3 29.7 all-gather.22
  130.8 43.8 all-gather.24
  182.7 29.7 all-gather.26
  215.2 43.8 all-gather.28
  268.3 69.0 all-gather.46
  367.2 27.9 all-gather.30
  398.0 43.8 all-gather.32
  449.7 29.7 all-gather.34
  482.4 43.8 all-gather.36
  534.3 29.7 all-gather.38
  567.0 43.8 all-gather.40
  620.0 69.0 all-gather.48
  718.9 27.9 all-gather.42
  749.5 43.8 all-gather.44
  801.5 138.7 all-reduce.1
